TPU v7x, 256 devices: a whole 4x4x8 slice. The times are simulated.
256 devices in a mesh: dp: 8 (over x, z_lo), seq: 32 (over z_hi, y, core).
Axes of the slice: x: 4, y: 4, z: 8 (z_hi: 4, z_lo: 2; z = z_hi * 2 + z_lo), core: 2. Of those that a mesh axis runs over, the one named last changes fastest.
Arguments:
- tower_grad: bfloat16 [8192, 768], P(None, ('dp', 'seq')), may hold values from -6 to 6
- act_mid: bfloat16 [16384, 704], P('seq'), may hold values from -6 to 6
- pre_mid: bfloat16 [16384, 768], P('seq', 'dp'), may hold values from -6 to 6
- act_low: bfloat16 [32768, 640], P('seq'), may hold values from -6 to 6
- pre_low: bfloat16 [32768, 704], P('seq', 'dp'), may hold values from -6 to 6
- weight_upper: bfloat16 [5, 704, 768], P(None, 'seq', 'dp'), may hold values from -0.109375 to 0.109375
- weight_lower: bfloat16 [5, 640, 704], P(None, 'seq', 'dp'), may hold values from -0.109375 to 0.109375
Outputs:
- grad_low_act: bfloat16 [32768, 640], P('seq', 'dp')
- grad_upper: float32 [5, 704, 768], P(None, 'seq', 'dp')
- grad_lower: float32 [5, 640, 704], P(None, 'seq', 'dp')
All inputs are finite; a program needn't handle non-finite values.
Results may differ from a plain program's by a relative error of at most 0.0065.
Values may be sent and summed in bfloat16 or wider, within the bound.
No kernel may reach another device: no remote copies, remote signals or barrier semaphores. Data moves between devices by JAX's collectives and lax.ppermute only.
A program may use at most 64 MiB of HBM per device.

v0:
```python
import math
import jax
import jax.numpy as jnp
from jax import lax
from jax.sharding import PartitionSpec as P

KWIDTH = 5


def with_halo(block, sides, width):
    for axis, dim in sides:
        count = lax.axis_size(axis)
        forward = [(i, i + 1) for i in range(count - 1)]
        backward = [(target, source) for source, target in forward]
        low = lax.ppermute(
            lax.slice_in_dim(block, block.shape[dim] - width, None, axis=dim), axis, forward
        )
        high = lax.ppermute(lax.slice_in_dim(block, 0, width, axis=dim), axis, backward)
        block = jnp.concatenate([low, block, high], axis=dim)
    return block


def gelu_slope(pre_act):
    values = pre_act.astype(jnp.float32)
    cumulative = 0.5 * (1.0 + lax.erf(values * (1.0 / math.sqrt(2.0))))
    density = jnp.exp(-0.5 * values * values) * (1.0 / math.sqrt(2.0 * math.pi))
    return cumulative + values * density


def level_back(upper_grad, act, pre_act, weight):
    rows = act.shape[0]
    half = KWIDTH // 2
    spread = jnp.repeat(upper_grad.astype(jnp.float32), 2, axis=0) * 0.5
    pre_grad = (spread * gelu_slope(pre_act)).astype(jnp.bfloat16)
    padded = with_halo(pre_grad, (("seq", 0),), half)
    act_grad = jnp.zeros((rows, weight.shape[1]), jnp.float32)
    pieces = []
    for offset in range(KWIDTH):
        begin = 2 * half - offset
        shifted = padded[begin : begin + rows]
        pieces.append(jnp.einsum("si,so->io", act, shifted, preferred_element_type=jnp.float32))
        act_grad = act_grad + jnp.einsum(
            "so,io->si", shifted, weight[offset], preferred_element_type=jnp.float32
        )
    return (act_grad, jnp.stack(pieces))


def local(tower_grad, act_mid, pre_mid, act_low, pre_low, weight_upper, weight_lower):
    upper_full, lower_full = (
        lax.all_gather(weight_upper, "seq", axis=1, tiled=True),
        lax.all_gather(weight_lower, "seq", axis=1, tiled=True),
    )
    slab_grad = lax.all_to_all(tower_grad, "seq", split_axis=0, concat_axis=1, tiled=True)
    mid_part, upper_part = level_back(slab_grad, act_mid, pre_mid, upper_full)
    mid_total = act_mid.shape[0] * lax.axis_size("seq")
    low_total = act_low.shape[0] * lax.axis_size("seq")
    upper_term = upper_part * (1.0 / math.sqrt(mid_total))
    mid_summed = lax.psum(mid_part, "dp")
    share_width = pre_low.shape[1]
    mid_own = lax.dynamic_slice_in_dim(
        mid_summed, lax.axis_index("dp") * share_width, share_width, 1
    )
    low_part, lower_part = level_back(mid_own.astype(jnp.bfloat16), act_low, pre_low, lower_full)
    lower_term = lower_part * (1.0 / math.sqrt(low_total))
    grad_upper, grad_lower = (
        lax.psum_scatter(upper_term, "seq", scatter_dimension=1, tiled=True),
        lax.psum_scatter(lower_term, "seq", scatter_dimension=1, tiled=True),
    )
    low_grad = lax.psum_scatter(low_part, "dp", scatter_dimension=1, tiled=True)
    return (low_grad.astype(jnp.bfloat16), grad_upper, grad_lower)


def solution(mesh):
    in_specs = (
        P(None, ("dp", "seq")),
        P("seq", None),
        P("seq", "dp"),
        P("seq", None),
        P("seq", "dp"),
        P(None, "seq", "dp"),
        P(None, "seq", "dp"),
    )
    out_specs = (P("seq", "dp"), P(None, "seq", "dp"), P(None, "seq", "dp"))
    return jax.shard_map(local, mesh=mesh, in_specs=in_specs, out_specs=out_specs, check_vma=False)
```

profile of v0, /device:TPU:1, one launch (start us, length us, event | category | flops | bytes accessed | tf_op | source)
XLA Modules:
  0.0 443.1 jit_solution(7031288359553033006)
XLA Ops:
  7.2 13.0 %all-to-all-start = ((bf16[32,256,3]{1,2,0:T(4,128)(2,1)}), bf16[32,256,3]{1,2,0:T(4,128)(2,1)}, u32[]{:S(2)}, u32[]{:S(2)}) async-start(bf16[32,256,3]{1,2,0:T(4,128)(2,1)} %bitcast.113), calls=%async_computation | async-start | bytes 131072 | tf_op jit(solution)/shard_map/all_to_all | solution.py:53
  20.2 0.8 copy.33
  21.0 50.7 %all_gather.6 = bf16[5,704,96]{2,0,1:T(8,128)(2,1)S(1)} all-gather(bf16[5,22,96]{2,0,1:T(8,128)(2,1)S(1)} %copy.33), channel_id=1, replica_groups=mesh['dp'=8,'seq'=32] {'seq'}, dimensions={1}, use_global_device_ids=true | all-gather | bytes 696960 | tf_op jit(solution)/shard_map/all_gather | solution.py:50
  71.7 1.3 fusion.66
  73.8 1.1 copy.40
  74.9 0.8 copy.54
  75.7 0.8 copy.53
  76.5 0.8 copy.52
  77.3 0.8 copy.51
  78.1 0.8 copy.55
  78.9 0.9 multiply_bitcast_fusion
  80.2 2.1 collective-permute-start
  82.3 3.5 collective-permute-start.1
  88.2 68.9 %all-reduce.1 = bf16[512,704]{0,1:T(8,128)(2,1)} all-reduce(f32[512,704]{0,1:T(8,128)S(1)} %fusion), channel_id=1, replica_groups=mesh['dp'=8,'seq'=32] {'dp'}, use_global_device_ids=true, to_apply=%region_0.0 | all-reduce | flops 360448 | bytes 2162688 | tf_op jit(solution)/shard_map/psum | solution.py:58
  157.2 0.9 convert_multiply_fusion.8
  158.7 10.5 %collective-permute-start.2 = (bf16[2,88]{1,0:T(2,128)(2,1)S(1)}, bf16[2,88]{1,0:T(2,128)(2,1)S(1)}, u32[]{:S(2)}, u32[]{:S(2)}) collective-permute-start(bf16[2,88]{1,0:T(2,128)(2,1)S(1)} %get-tuple-element.25), channel_id=1, source_target_pairs={{1,0},{2,1},{3,2},{4,3},{5,4},{6,5},{7,6},{8,7},{9,8},{10,9},{11,1... | collective-permute-start | bytes 1064 | tf_op jit(solution)/shard_map/ppermute | solution.py:18
  169.2 4.2 collective-permute-start.3
  175.4 2.2 copy.48
  177.7 48.1 %all_gather.7 = bf16[5,640,88]{2,0,1:T(8,128)(2,1)} all-gather(bf16[5,20,88]{2,0,1:T(8,128)(2,1)S(1)} %copy.41), channel_id=1, replica_groups=mesh['dp'=8,'seq'=32] {'seq'}, dimensions={1}, use_global_device_ids=true | all-gather | bytes 580800 | tf_op jit(solution)/shard_map/all_gather | solution.py:51
  227.8 2.2 copy.47
  230.2 1.2 copy-done.2
  231.5 2.1 fusion.67
  233.6 1.1 copy.60
  234.7 1.1 copy.59
  235.9 1.1 copy.58
  239.6 2.2 add_add_fusion
  241.8 30.1 %reduce-scatter.8.cloned.1.call-done = f32[5,20,88]{2,0,1:T(8,128)} async-done(((f32[5,640,88]{2,0,1:T(8,128)}), f32[5,20,88]{2,0,1:T(8,128)}) %reduce-scatter.8.cloned.1.call-update) | async-done | bytes 35216 | tf_op jit(solution)/shard_map/reduce_scatter | solution.py:67
  271.9 1.5 copy.50
  273.5 95.1 %reduce-scatter.6.cloned.1.call-done = f32[5,22,96]{2,0,1:T(8,128)} async-done(((f32[5,704,96]{2,0,1:T(8,128)}), f32[5,22,96]{2,0,1:T(8,128)}) %reduce-scatter.6.cloned.1.call-update) | async-done | bytes 42256 | tf_op jit(solution)/shard_map/reduce_scatter | solution.py:66
  368.5 1.5 copy.49
  370.1 64.8 %reduce-scatter.4.cloned.1.call-done = f32[1024,80]{0,1:T(8,128)} async-done(((f32[1024,640]{0,1:T(8,128)}), f32[1024,80]{0,1:T(8,128)}) %reduce-scatter.4.cloned.1.call-update) | async-done | bytes 327696 | tf_op jit(solution)/shard_map/reduce_scatter | solution.py:69
  434.9 1.7 convert_element_type.33
  (64 shorter events, 10.9 us)
Async XLA Ops:
  7.2 166.2 %copy-start = (bf16[1024,640]{1,0:T(8,128)(2,1)S(1)}, bf16[1024,640]{1,0:T(8,128)(2,1)}, u32[]{:S(2)}) copy-start(bf16[1024,640]{1,0:T(8,128)(2,1)} %param.10) | copy-start | bytes 3932164
  7.2 71.8 %all-to-all-start = ((bf16[32,256,3]{1,2,0:T(4,128)(2,1)}), bf16[32,256,3]{1,2,0:T(4,128)(2,1)}, u32[]{:S(2)}, u32[]{:S(2)}) async-start(bf16[32,256,3]{1,2,0:T(4,128)(2,1)} %bitcast.113), calls=%async_computation | async-start | bytes 131072 | tf_op jit(solution)/shard_map/all_to_all | solution.py:53
  20.1 251.8 %reduce-scatter.8.cloned.1.call-start = ((), (), s32[]{:S(2)}) async-start(), calls=%async_computation.6 | async-start | bytes 2703360 | tf_op jit(solution)/shard_map/reduce_scatter | solution.py:67
  71.7 1.3 copy-start.4
  75.7 4.4 copy-start.3
  80.2 6.7 %collective-permute-start = (bf16[2,96]{1,0:T(2,128)(2,1)S(1)}, bf16[2,96]{1,0:T(2,128)(2,1)S(1)}, u32[]{:S(2)}, u32[]{:S(2)}) collective-permute-start(bf16[2,96]{1,0:T(2,128)(2,1)S(1)} %get-tuple-element.27), channel_id=1, source_target_pairs={{1,0},{2,1},{3,2},{4,3},{5,4},{6,5},{7,6},{8,7},{9,8},{10,9},{11,1... | collective-permute-start | bytes 1160 | tf_op jit(solution)/shard_map/ppermute | solution.py:18
  82.3 4.2 collective-permute-start.1
  86.5 1.3 copy-start.6
  86.9 0.5 copy-start.8
  157.2 12.0 %copy-start.5 = (bf16[5,20,88]{2,1,0:T(8,128)(2,1)S(1)}, bf16[5,20,88]{2,1,0:T(8,128)(2,1)}, u32[]{:S(2)}) copy-start(bf16[5,20,88]{2,1,0:T(8,128)(2,1)} %param.13) | copy-start | bytes 52804
  158.7 14.7 %collective-permute-start.2 = (bf16[2,88]{1,0:T(2,128)(2,1)S(1)}, bf16[2,88]{1,0:T(2,128)(2,1)S(1)}, u32[]{:S(2)}, u32[]{:S(2)}) collective-permute-start(bf16[2,88]{1,0:T(2,128)(2,1)S(1)} %get-tuple-element.25), channel_id=1, source_target_pairs={{1,0},{2,1},{3,2},{4,3},{5,4},{6,5},{7,6},{8,7},{9,8},{10,9},{11,1... | collective-permute-start | bytes 1064 | tf_op jit(solution)/shard_map/ppermute | solution.py:18
  169.2 5.4 %collective-permute-start.3 = (bf16[2,88]{1,0:T(2,128)(2,1)S(1)}, bf16[2,88]{1,0:T(2,128)(2,1)S(1)}, u32[]{:S(2)}, u32[]{:S(2)}) collective-permute-start(bf16[2,88]{1,0:T(2,128)(2,1)S(1)} %get-tuple-element.26), channel_id=1, source_target_pairs={{0,1},{1,2},{2,3},{3,4},{4,5},{5,6},{6,7},{7,8},{8,9},{9,10},{10,1... | collective-permute-start | bytes 1064 | tf_op jit(solution)/shard_map/ppermute | solution.py:15
  177.6 48.2 %copy-start.1 = (bf16[512,704]{0,1:T(8,128)(2,1)S(1)}, bf16[512,704]{0,1:T(8,128)(2,1)}, u32[]{:S(2)}) copy-start(bf16[512,704]{0,1:T(8,128)(2,1)} %param.8) | copy-start | bytes 2162692
  177.6 48.2 %copy-start.9 = (bf16[2,96]{1,0:T(2,128)(2,1)S(1)}, bf16[2,96]{1,0:T(2,128)(2,1)}, u32[]{:S(2)}) copy-start(bf16[2,96]{1,0:T(2,128)(2,1)} %copy-done.8) | copy-start | bytes 1156
  177.6 190.9 %reduce-scatter.6.cloned.1.call-start = ((), (), s32[]{:S(2)}) async-start(), calls=%async_computation.5 | async-start | bytes 2973696 | tf_op jit(solution)/shard_map/reduce_scatter | solution.py:66
  225.8 1.1 copy-start.7
  230.0 1.5 copy-start.2
  230.0 204.9 %reduce-scatter.4.cloned.1.call-start = ((), (), s32[]{:S(2)}) async-start(), calls=%async_computation.4 | async-start | bytes 2949120 | tf_op jit(solution)/shard_map/reduce_scatter | solution.py:69
Sparse Core Ops, SparseCore 0:
  177.7 94.1 reduce-scatter.7
  276.3 92.1 reduce-scatter.5
  371.1 63.7 reduce-scatter.3
where the time goes:
time: 444 us; the launch traced here: 443 us
  waiting for transfers between devices  190 us (43%)
  blocking collectives  168 us (38%)
  starting transfers between devices  33.5 us (8%)
  local copies, waits for them, and re-layouts  23.2 us (5%)
  between operations  14.2 us (3%)
  matrix products  10 us (2%)
    reduce_scatter x1, waiting for transfers between devices, local(): lax.psum_scatter(upper_term, 'seq', scatter_dimension=1, tiled=True)  95.1 us
    psum x1, blocking collectives, local(): mid_summed = lax.psum(mid_part, 'dp')  68.9 us
    reduce_scatter x1, waiting for transfers between devices, local(): low_grad = lax.psum_scatter(low_part, 'dp', scatter_dimension=1, tiled=True)  64.8 us
    all_gather x1, blocking collectives, local(): lax.all_gather(weight_upper, 'seq', axis=1, tiled=True)  50.7 us
    all_gather x1, blocking collectives, local(): lax.all_gather(weight_lower, 'seq', axis=1, tiled=True)  48.1 us
    reduce_scatter x1, waiting for transfers between devices, local(): lax.psum_scatter(lower_term, 'seq', scatter_dimension=1, tiled=True)  30.1 us
    unnamed x36, local copies, waits for them, and re-layouts  14.8 us
    all_to_all x1, starting transfers between devices, local(): lax.all_to_all(tower_grad, 'seq', split_axis=0, concat_axis=1, tiled=True)  13 us
  transfers between devices with their start and end apart: 8, of which 4 were waited for; matrix products, arithmetic and copies ran while one was open for 6% of the time, Pallas kernels for 0%

commit v1 on v0

--- a/solution.py
+++ b/solution.py
@@ -55,7 +55,7 @@
     mid_total = act_mid.shape[0] * lax.axis_size("seq")
     low_total = act_low.shape[0] * lax.axis_size("seq")
     upper_term = upper_part * (1.0 / math.sqrt(mid_total))
-    mid_summed = lax.psum(mid_part, "dp")
+    mid_summed = jnp.sum(lax.all_gather(mid_part, "dp"), axis=0)
     share_width = pre_low.shape[1]
     mid_own = lax.dynamic_slice_in_dim(
         mid_summed, lax.axis_index("dp") * share_width, share_width, 1

time: 444 us -> 551 us (1.24)
  waiting for transfers between devices: 190 us -> 347 us
  blocking collectives: 168 us -> 99.1 us
  local copies, waits for them, and re-layouts: 23.2 us -> 43.1 us
  starting transfers between devices: 33.5 us -> 24.4 us
  other arithmetic: 4.06 us -> 9.6 us
    all_gather x0 -> x1, waiting for transfers between devices: none -> 190 us  [local(): mid_summed = jnp.sum(lax.all_gather(mid_part, 'dp'), axis=0)]
    reduce_scatter x1, waiting for transfers between devices: 95.1 us -> 0.03 us  [local(): lax.psum_scatter(upper_term, 'seq', scatter_dimension=1, tiled=True)]
    psum x1 -> x0, blocking collectives: 68.9 us -> none  [local(): mid_summed = lax.psum(mid_part, 'dp')]
    reduce_scatter x1, waiting for transfers between devices: 30.1 us -> 91 us  [local(): lax.psum_scatter(lower_term, 'seq', scatter_dimension=1, tiled=True)]
    unnamed x36 -> x37, local copies, waits for them, and re-layouts: 14.8 us -> 34.9 us
    ppermute x2, starting transfers between devices: 12.5 us -> 4.65 us  [with_halo(): lax.ppermute(lax.slice_in_dim(block, 0, width, axis=dim), axis, backward)]
    reduce_sum x0 -> x1, other arithmetic: none -> 7.27 us  [local(): mid_summed = jnp.sum(lax.all_gather(mid_part, 'dp'), axis=0)]
  transfers between devices with their start and end apart: 8 -> 9, of which waited for: 4 -> 4; matrix products, arithmetic and copies ran while one was open for 6% -> 10% of each run, Pallas kernels for 0% -> 0%
where the time goes in v1:
time: 551 us; the launch traced here: 550 us
  waiting for transfers between devices  347 us (63%)
  blocking collectives  99.1 us (18%)
  local copies, waits for them, and re-layouts  43.1 us (8%)
  starting transfers between devices  24.4 us (4%)
  between operations  16 us (3%)
  matrix products  11.2 us (2%)
  other arithmetic  9.6 us (2%)
    all_gather x1, waiting for transfers between devices, local(): mid_summed = jnp.sum(lax.all_gather(mid_part, 'dp'), axis=0)  190 us
    reduce_scatter x1, waiting for transfers between devices, local(): lax.psum_scatter(lower_term, 'seq', scatter_dimension=1, tiled=True)  91 us
    reduce_scatter x1, waiting for transfers between devices, local(): low_grad = lax.psum_scatter(low_part, 'dp', scatter_dimension=1, tiled=True)  64.8 us
    all_gather x1, blocking collectives, local(): lax.all_gather(weight_upper, 'seq', axis=1, tiled=True)  50.8 us
    all_gather x1, blocking collectives, local(): lax.all_gather(weight_lower, 'seq', axis=1, tiled=True)  48.3 us
    unnamed x37, local copies, waits for them, and re-layouts  34.9 us
    all_to_all x1, starting transfers between devices, local(): lax.all_to_all(tower_grad, 'seq', split_axis=0, concat_axis=1, tiled=True)  12.9 us
  transfers between devices with their start and end apart: 9, of which 4 were waited for; matrix products, arithmetic and copies ran while one was open for 10% of the time, Pallas kernels for 0%

profile of v1, /device:TPU:1, one launch (start us, length us, event | category | flops | bytes accessed | tf_op | source)
XLA Modules:
  0.0 550.2 jit_solution(16734197547740259835)
XLA Ops:
  8.0 12.9 %all-to-all-start = ((bf16[32,256,3]{1,2,0:T(4,128)(2,1)}), bf16[32,256,3]{1,2,0:T(4,128)(2,1)S(1)}, u32[]{:S(2)}, u32[]{:S(2)}) async-start(bf16[32,256,3]{1,2,0:T(4,128)(2,1)} %bitcast.119), calls=%async_computation | async-start | bytes 131072 | tf_op jit(solution)/shard_map/all_to_all | solution.py:53
  21.0 0.8 copy.32
  21.7 50.8 %all_gather.12 = bf16[5,704,96]{2,0,1:T(8,128)(2,1)S(1)} all-gather(bf16[5,22,96]{2,0,1:T(8,128)(2,1)S(1)} %copy.32), channel_id=1, replica_groups=mesh['dp'=8,'seq'=32] {'seq'}, dimensions={1}, use_global_device_ids=true | all-gather | bytes 696960 | tf_op jit(solution)/shard_map/all_gather | solution.py:50
  72.6 1.3 fusion.66
  74.0 0.8 copy.51
  74.8 0.8 copy.52
  75.6 0.8 copy.50
  76.4 0.8 copy.54
  77.2 0.8 copy.53
  78.5 2.1 collective-permute-start
  81.0 3.5 collective-permute-start.1
  86.0 1.6 fusion
  87.6 0.8 copy-done.7
  88.4 0.8 copy.39
  89.3 48.3 %all_gather.15 = bf16[5,640,88]{2,0,1:T(8,128)(2,1)S(1)} all-gather(bf16[5,20,88]{2,0,1:T(8,128)(2,1)S(1)} %copy.40), channel_id=1, replica_groups=mesh['dp'=8,'seq'=32] {'seq'}, dimensions={1}, use_global_device_ids=true | all-gather | bytes 580800 | tf_op jit(solution)/shard_map/all_gather | solution.py:51
  137.6 2.0 fusion.67
  139.7 1.8 copy.56
  141.4 0.8 copy.55
  144.2 2.2 copy.46
  146.7 190.5 %all-gather.3.cloned.1.call-done = f32[4096,704]{0,1:T(8,128)} async-done(((f32[512,704]{0,1:T(8,128)}), f32[4096,704]{0,1:T(8,128)}) %all-gather.3.cloned.1.call-update) | async-done | bytes 11534352 | tf_op jit(solution)/shard_map/all_gather | solution.py:58
  337.2 19.9 %copy.60 = f32[88,8,8,512]{3,2,1,0:T(8,128)} copy(f32[88,8,8,512]{3,1,2,0:T(8,128)} %bitcast.116) | data formatting | bytes 23068672
  357.1 7.3 %bitcast_reduce_fusion = bf16[512,704]{0,1:T(8,128)(2,1)S(1)} fusion(f32[88,8,8,512]{3,2,1,0:T(8,128)} %copy.60), kind=kLoop, calls=%fused_computation | loop fusion | flops 2523136 | bytes 12255232 | tf_op jit(solution)/shard_map/reduce_sum | solution.py:58
  365.6 2.6 collective-permute-start.2
  368.4 0.8 copy.58
  369.3 3.0 collective-permute-start.3
  374.4 2.1 copy.47
  379.8 2.3 add_add_fusion
  382.1 1.5 copy.48
  383.6 91.0 %reduce-scatter.8.cloned.1.call-done = f32[5,20,88]{2,0,1:T(8,128)} async-done(((f32[5,640,88]{2,0,1:T(8,128)}), f32[5,20,88]{2,0,1:T(8,128)}) %reduce-scatter.8.cloned.1.call-update) | async-done | bytes 35216 | tf_op jit(solution)/shard_map/reduce_scatter | solution.py:67
  474.7 1.5 copy.49
  476.2 64.8 %reduce-scatter.4.cloned.1.call-done = f32[1024,80]{0,1:T(8,128)} async-done(((f32[1024,640]{0,1:T(8,128)}), f32[1024,80]{0,1:T(8,128)}) %reduce-scatter.4.cloned.1.call-update) | async-done | bytes 327696 | tf_op jit(solution)/shard_map/reduce_scatter | solution.py:69
  541.0 1.7 convert_element_type.33
  (68 shorter events, 11.4 us)
Async XLA Ops:
  8.0 364.4 %copy-start = (bf16[1024,640]{1,0:T(8,128)(2,1)S(1)}, bf16[1024,640]{1,0:T(8,128)(2,1)}, u32[]{:S(2)}) copy-start(bf16[1024,640]{1,0:T(8,128)(2,1)} %param.10) | copy-start | bytes 3932164
  8.0 70.0 %all-to-all-start = ((bf16[32,256,3]{1,2,0:T(4,128)(2,1)}), bf16[32,256,3]{1,2,0:T(4,128)(2,1)S(1)}, u32[]{:S(2)}, u32[]{:S(2)}) async-start(bf16[32,256,3]{1,2,0:T(4,128)(2,1)} %bitcast.119), calls=%async_computation | async-start | bytes 131072 | tf_op jit(solution)/shard_map/all_to_all | solution.py:53
  20.9 316.3 %all-gather.3.cloned.1.call-start = ((), (), s32[]{:S(2)}) async-start(), calls=%async_computation.7 | async-start | bytes 12976128 | tf_op jit(solution)/shard_map/all_gather | solution.py:58
  72.6 1.3 copy-start.8
  78.5 6.0 %collective-permute-start = (bf16[2,96]{1,0:T(2,128)(2,1)S(1)}, bf16[2,96]{1,0:T(2,128)(2,1)S(1)}, u32[]{:S(2)}, u32[]{:S(2)}) collective-permute-start(bf16[2,96]{1,0:T(2,128)(2,1)S(1)} %get-tuple-element.27), channel_id=1, source_target_pairs={{1,0},{2,1},{3,2},{4,3},{5,4},{6,5},{7,6},{8,7},{9,8},{10,9},{11,1... | collective-permute-start | bytes 1160 | tf_op jit(solution)/shard_map/ppermute | solution.py:18
  81.0 4.2 collective-permute-start.1
  87.5 0.9 copy-start.7
  87.5 1.8 copy-start.9
  87.5 294.5 %reduce-scatter.6.cloned.1.call-start = ((), (), s32[]{:S(2)}) async-start(), calls=%async_computation.5 | async-start | bytes 2973696 | tf_op jit(solution)/shard_map/reduce_scatter | solution.py:66
  137.6 4.6 copy-start.1
  146.5 328.2 %reduce-scatter.8.cloned.1.call-start = ((), (), s32[]{:S(2)}) async-start(), calls=%async_computation.6 | async-start | bytes 2703360 | tf_op jit(solution)/shard_map/reduce_scatter | solution.py:67
  364.4 1.0 copy-start.3
  364.4 3.8 copy-start.2
  365.6 6.7 %collective-permute-start.2 = (bf16[2,88]{1,0:T(2,128)(2,1)S(1)}, bf16[2,88]{1,0:T(2,128)(2,1)S(1)}, u32[]{:S(2)}, u32[]{:S(2)}) collective-permute-start(bf16[2,88]{1,0:T(2,128)(2,1)S(1)} %get-tuple-element.25), channel_id=1, source_target_pairs={{1,0},{2,1},{3,2},{4,3},{5,4},{6,5},{7,6},{8,7},{9,8},{10,9},{11,1... | collective-permute-start | bytes 1064 | tf_op jit(solution)/shard_map/ppermute | solution.py:18
  369.3 4.1 collective-permute-start.3
  376.5 0.9 copy-start.4
  376.5 164.5 %reduce-scatter.4.cloned.1.call-start = ((), (), s32[]{:S(2)}) async-start(), calls=%async_computation.4 | async-start | bytes 2949120 | tf_op jit(solution)/shard_map/reduce_scatter | solution.py:69
  377.4 0.9 copy-start.5
  378.3 0.9 copy-start.6
Sparse Core Ops, SparseCore 0:
  87.7 249.4 all-gather.2
Sparse Core Ops, SparseCore 1:
  146.6 205.3 reduce-scatter.5
  376.6 98.0 reduce-scatter.7
  477.1 63.8 reduce-scatter.3
